TPU v7x, 32 devices: a whole 2x2x4 slice. The times are simulated.
32 devices in a mesh: rep: 2 (over x), node: 2 (over core), local: 8 (over z, y).
Axes of the slice: x: 2, y: 2, z: 4, core: 2. Of those that a mesh axis runs over, the one named last changes fastest.
Arguments:
- tokens: bfloat16 [1024, 3584], P(('rep', 'node', 'local')), parts along dimension 0, may hold values from -6 to 6
- expert_ids: int32 [1024, 8], P(('rep', 'node', 'local')), parts along dimension 0, may hold values from 0 to 15, all different within a row; in each aligned block of 32 rows (0 to 31, 32 to 63, ...) at most 32 rows name the same one
- route_weights: bfloat16 [1024, 8], P(('rep', 'node', 'local')), parts along dimension 0, may hold values from 0.099609375 to 1
- w_up: bfloat16 [16, 3584, 1024], P(('node', 'local')), may hold values from -0.09375 to 0.09375
- w_down: bfloat16 [16, 1024, 3584], P(('node', 'local')), may hold values from -0.1875 to 0.1875
Outputs:
- mixed: bfloat16 [1024, 3584], P(('rep', 'node', 'local')), parts along dimension 0
There are 2 independent parts, one for each index of `rep`. A program takes and returns all parts, laid end to end along the dimension named above; an argument that names none is the same for every part. Nothing has to cross between parts.
Inputs may be any that keep to these rules, and one draw needn't show every extreme that they name: `expert_ids`: the 8 experts of a token differ; in each aligned block of 32 rows (the rows of one device) no expert is named by more than 32 rows.
All inputs are finite; a program needn't handle non-finite values.
Results may differ from a plain program's by a relative error of at most 0.0058.
Values may be sent and summed in bfloat16 or wider, within the bound.
A program may use at most 64 MiB of HBM per device.

v0:
```python
import jax
import jax.numpy as jnp
from jax import lax
from jax.sharding import PartitionSpec as P


def place_rows(targets, groups, width):
    onehot = (targets[:, None] == jnp.arange(groups, dtype=jnp.int32)[None, :]).astype(jnp.int32)
    before = jnp.cumsum(onehot, axis=0) - onehot
    rank = jnp.sum(before * onehot, axis=1)
    return jnp.where(targets >= 0, targets * width + rank, groups * width)


def per_device(tokens, expert_ids, route_weights, w_up, w_down):
    up_matrix = w_up[0]
    down_matrix = w_down[0]
    rows = tokens.shape[0]
    top = expert_ids.shape[1]
    width_d = tokens.shape[1]
    experts = lax.axis_size(("node", "local"))
    most = max(4, 2 * rows * top // experts)
    slot = place_rows(expert_ids.reshape(-1), experts, most)
    source = tokens[jnp.arange(rows * top, dtype=jnp.int32) // top]
    buffer = jnp.zeros((experts * most, width_d), jnp.bfloat16).at[slot].set(source, mode="drop")
    buffer = buffer.reshape(experts, most, width_d)
    received = lax.all_to_all(buffer, ("node", "local"), split_axis=0, concat_axis=0, tiled=True)
    shape = received.shape
    flat = received.reshape(-1, shape[-1])
    hidden = jax.nn.silu(jnp.dot(flat, up_matrix, preferred_element_type=jnp.float32)).astype(
        jnp.bfloat16
    )
    answer = jnp.dot(hidden, down_matrix, preferred_element_type=jnp.float32).astype(jnp.bfloat16)
    done = answer.reshape(shape)
    returned = lax.all_to_all(
        done, ("node", "local"), split_axis=0, concat_axis=0, tiled=True
    ).reshape(experts * most, width_d)
    picked = returned[jnp.minimum(slot, experts * most - 1)].reshape(rows, top, width_d)
    mixed = jnp.einsum("tk,tkd->td", route_weights, picked, preferred_element_type=jnp.float32)
    return mixed.astype(jnp.bfloat16)


def solution(mesh):
    placed = (
        P(("rep", "node", "local"), None),
        P(("rep", "node", "local"), None),
        P(("rep", "node", "local"), None),
        P(("node", "local"), None, None),
        P(("node", "local"), None, None),
    )
    return jax.shard_map(
        per_device,
        mesh=mesh,
        in_specs=placed,
        out_specs=P(("rep", "node", "local"), None),
        check_vma=False,
    )
```

profile of v0, /device:TPU:0, one launch (start us, length us, event | category | flops | bytes accessed | tf_op | source)
XLA Modules:
  0.0 212.5 jit_solution(13505756013356486724)
XLA Ops:
  0.0 0.0 copy-start
  0.0 0.8 copy.8
  0.8 0.1 eq.29
  0.9 0.1 eq.25
  1.0 0.7 broadcast_multiply_fusion
  1.7 0.7 broadcast_compare_fusion
  2.4 0.6 reduce-window.6
  3.0 0.2 slice_reduce_fusion
  3.2 0.1 copy.7
  3.3 0.1 mul.25
  3.4 0.1 copy.6
  3.5 0.1 ge.18
  3.6 0.1 fusion.18
  3.7 0.0 copy-done
  3.7 10.9 %scatter_custom_fusion = bf16[512,3584]{1,0:T(8,128)(2,1)} fusion(s32[256]{0:T(256)S(1)} %bitcast.55, bf16[32,3584]{1,0:T(8,128)(2,1)S(1)} %copy-done, s32[1024]{0:T(1024)S(1)} %pad_clamp_fusion.1, bf16[]{:T(256)} %constant.26.clone.1), kind=kCustom, calls=%fused_computation.11 | custom fusion | bytes 3670018 | tf_op jit(solution)/shard_map/scatter | solution.py:24
  14.6 90.7 %all_to_all.10 = bf16[16,32,3584]{2,1,0:T(8,128)(2,1)} all-to-all(bf16[16,32,3584]{2,1,0:T(8,128)(2,1)} %bitcast.48), channel_id=1, replica_groups=mesh['rep'=2,'node'=2,'local'=8] {'node','local'}, dimensions={0} | all-to-all | bytes 7340032 | tf_op jit(solution)/shard_map/all_to_all | solution.py:26
  105.3 16.0 %fusion.4 = bf16[512,3584]{1,0:T(8,128)(2,1)} fusion(bf16[1,1024,3584]{2,1,0:T(8,128)(2,1)} %param.9, bf16[512,3584]{1,0:T(8,128)(2,1)} %bitcast.50, bf16[1,3584,1024]{2,1,0:T(8,128)(2,1)} %param.8), kind=kOutput, calls=%fused_computation.7 | convolution fusion | flops 7520649216 | bytes 22020096 | tf_op jit(solution)/shard_map/dot_general | solution.py:32
  121.3 0.0 copy-start.1
  121.3 4.6 %all-to-all-start.1 = ((bf16[16,32,3584]{2,1,0:T(8,128)(2,1)}), bf16[16,32,3584]{2,1,0:T(8,128)(2,1)}, u32[]{:S(2)}, u32[]{:S(2)}) async-start(bf16[16,32,3584]{2,1,0:T(8,128)(2,1)} %bitcast.49), calls=%async_computation.1 | async-start | bytes 7340032 | tf_op jit(solution)/shard_map/all_to_all | solution.py:34
  125.9 0.0 copy-done.1
  125.9 0.1 copy.11
  126.0 79.1 %all-to-all-done.1 = bf16[16,32,3584]{2,1,0:T(8,128)(2,1)} async-done(((bf16[16,32,3584]{2,1,0:T(8,128)(2,1)}), bf16[16,32,3584]{2,1,0:T(8,128)(2,1)}, u32[]{:S(2)}, u32[]{:S(2)}) %all-to-all-start.1) | async-done | bytes 3670048 | tf_op jit(solution)/shard_map/all_to_all | solution.py:34
  205.1 6.0 %gather_fusion = bf16[256,3584]{1,0:T(8,128)(2,1)S(1)} fusion(bf16[512,3584]{1,0:T(8,128)(2,1)} %bitcast.9, s32[1024]{0:T(1024)S(1)} %pad_clamp_fusion), kind=kCustom, calls=%fused_computation.1 | custom fusion | bytes 3671040 | tf_op jit(solution)/shard_map/gather | solution.py:37
  211.2 0.6 fusion.7
  211.8 0.7 copy.16
  (7 shorter events, 0.1 us)
Async XLA Ops:
  0.0 3.7 %copy-start = (bf16[32,3584]{1,0:T(8,128)(2,1)S(1)}, bf16[32,3584]{1,0:T(8,128)(2,1)}, u32[]{:S(2)}) copy-start(bf16[32,3584]{1,0:T(8,128)(2,1)} %param.5) | copy-start | bytes 688132
  121.3 4.6 %copy-start.1 = (bf16[32,8]{0,1:T(8,128)(2,1)S(1)}, bf16[32,8]{0,1:T(8,128)(2,1)}, u32[]{:S(2)}) copy-start(bf16[32,8]{0,1:T(8,128)(2,1)} %param.7) | copy-start | bytes 1540
  121.3 83.8 %all-to-all-start.1 = ((bf16[16,32,3584]{2,1,0:T(8,128)(2,1)}), bf16[16,32,3584]{2,1,0:T(8,128)(2,1)}, u32[]{:S(2)}, u32[]{:S(2)}) async-start(bf16[16,32,3584]{2,1,0:T(8,128)(2,1)} %bitcast.49), calls=%async_computation.1 | async-start | bytes 7340032 | tf_op jit(solution)/shard_map/all_to_all | solution.py:34
where the time goes:
time: 215 us; the launch traced here: 213 us
  blocking collectives  90.7 us (42%)
  waiting for transfers between devices  79.1 us (37%)
  local copies, waits for them, and re-layouts  19.3 us (9%)
  matrix products  16.6 us (8%)
  starting transfers between devices  4.63 us (2%)
    all_to_all x1, blocking collectives, per_device(): lax.all_to_all(buffer, ('node', 'local'), split_axis=0, concat_axis=0, ti...  90.7 us
    all_to_all x1, waiting for transfers between devices, per_device(): lax.all_to_all(done, ('node', 'local'), split_axis=0, concat_axis=0, tile...  79.1 us
    dot_general x1, matrix products, per_device(): jnp.dot(hidden, down_matrix, preferred_element_type=jnp.float32)  16 us
    scatter x1, local copies, waits for them, and re-layouts, per_device(): jnp.zeros((experts * most, width_d), jnp.bfloat16).at[slot]  10.9 us
    gather x1, local copies, waits for them, and re-layouts, per_device(): returned[jnp.minimum(slot, experts * most - 1)].reshape(rows, top, width_d)  6.04 us
    all_to_all x1, starting transfers between devices, per_device(): lax.all_to_all(done, ('node', 'local'), split_axis=0, concat_axis=0, tile...  4.63 us
  transfers between devices with their start and end apart: 1, of which 1 were waited for; matrix products, arithmetic and copies ran while one was open for 0% of the time, Pallas kernels for 0%

commit v1 on v0

--- a/solution.py
+++ b/solution.py
@@ -1,7 +1,276 @@
+import functools
 import jax
 import jax.numpy as jnp
 from jax import lax
+from jax.experimental import pallas as pl
+from jax.experimental.pallas import tpu as pltpu
 from jax.sharding import PartitionSpec as P
+
+MESH = pl.DeviceIdType.MESH
+LANES = 128
+
+
+def moe_kernel(sizes, x_hbm, dense_hbm, up_hbm, down_hbm, out_ref,
+               xg, wg, up, down, acc, hid, wcol,
+               psend, pown, precv, ysend, yown, yrecv, zsend, zown, zrecv,
+               own_sem, up_sem, down_sem,
+               gz_s, gz_r, gy_s, gy_r, gp_s, gp_r,
+               rp_s, rp_r, ry_s, ry_r, rz_s, rz_r):
+    rows, major, chunks, width = sizes
+    core = lax.axis_index("node")
+    local = lax.axis_index("local")
+    z, y = local // 2, lax.rem(local, 2)
+    col_rows = major * rows
+    half = 2 * col_rows
+
+    def at_z(d):
+        return {"local": lax.rem(z + d, major) * 2 + y}
+
+    at_y = {"local": z * 2 + (1 - y)}
+    at_p = {"node": 1 - core}
+
+    barrier = pltpu.get_barrier_semaphore()
+    peers = [at_z(d) for d in range(1, major)] + [at_y, at_p]
+    for peer in peers:
+        pl.semaphore_signal(barrier, inc=1, device_id=peer, device_id_type=MESH)
+
+    def rows_of(c, yy, zz):
+        return pl.multiple_of(c * half + yy * col_rows + zz * rows, rows)
+
+    mine = rows_of(core, y, z)
+    own_x = pltpu.make_async_copy(x_hbm, xg.at[pl.ds(mine, rows), :], own_sem.at[0])
+    own_w = pltpu.make_async_copy(dense_hbm, wg.at[pl.ds(mine, rows), :], own_sem.at[1])
+    own_x.start()
+    own_w.start()
+
+    def cols(j):
+        return pl.ds(pl.multiple_of(j * width, width), width)
+
+    def up_copy(j):
+        return pltpu.make_async_copy(up_hbm.at[0, cols(j), :], up.at[cols(j), :], up_sem.at[j])
+
+    def down_copy(j):
+        return pltpu.make_async_copy(down_hbm.at[0, :, cols(j)], down.at[:, cols(j)], down_sem.at[j])
+
+    lax.fori_loop(0, chunks, lambda j, _: (up_copy(j).start(), 0)[1], 0)
+    lax.fori_loop(0, chunks, lambda j, _: (down_copy(j).start(), 0)[1], 0)
+
+    own_x.wait()
+    own_w.wait()
+    pl.semaphore_wait(barrier, len(peers))
+
+    def view(start, size, j):
+        if j is None:
+            return wg.at[pl.ds(start, size), :]
+        return xg.at[pl.ds(start, size), cols(j)]
+
+    def idx(j):
+        return chunks if j is None else j
+
+    def remote(src, dst, s, r, device):
+        return pltpu.make_async_remote_copy(
+            src_ref=src, dst_ref=dst, send_sem=s, recv_sem=r, device_id=device, device_id_type=MESH)
+
+    def gz_send(d, j):
+        v = view(mine, rows, j)
+        return remote(v, v, gz_s.at[d - 1, idx(j)], gz_r.at[d - 1, idx(j)], at_z(d))
+
+    def gz_recv(d, j):
+        v = view(rows_of(core, y, lax.rem(z + major - d, major)), rows, j)
+        return remote(v, v, gz_s.at[d - 1, idx(j)], gz_r.at[d - 1, idx(j)], at_z(d))
+
+    def gy(which, j):
+        v = view(rows_of(core, which, 0), col_rows, j)
+        return remote(v, v, gy_s.at[idx(j)], gy_r.at[idx(j)], at_y)
+
+    def gp(k, c, which, j):
+        v = view(rows_of(c, which, 0), col_rows, j)
+        return remote(v, v, gp_s.at[k, idx(j)], gp_r.at[k, idx(j)], at_p)
+
+    def stage0(j):
+        for d in range(1, major):
+            gz_send(d, j).start()
+
+    def stage1(j):
+        for d in range(1, major):
+            gz_recv(d, j).wait_recv()
+        gy(y, j).start()
+        gp(0, core, y, j).start()
+
+    def stage2(j):
+        gy(1 - y, j).wait_recv()
+        gp(1, core, 1 - y, j).start()
+
+    def stage3(j):
+        gp(0, 1 - core, y, j).wait_recv()
+        gp(1, 1 - core, 1 - y, j).wait_recv()
+
+    lax.fori_loop(0, chunks, lambda j, _: (stage0(j), 0)[1], 0)
+    stage0(None)
+
+    def gather_step(t, _):
+        @pl.when(t < chunks)
+        def _():
+            stage1(t)
+
+        @pl.when((t >= 1) & (t <= chunks))
+        def _():
+            stage2(t - 1)
+
+        @pl.when(t >= 2)
+        def _():
+            j = t - 2
+            stage3(j)
+            up_copy(j).wait()
+            for k in range(2):
+                r = pl.ds(k * half, half)
+                part = jnp.dot(xg[r, cols(j)], up[cols(j), :], preferred_element_type=jnp.float32)
+
+                @pl.when(j == 0)
+                def _():
+                    acc[r, :] = part
+
+                @pl.when(j > 0)
+                def _():
+                    acc[r, :] += part
+        return 0
+
+    lax.fori_loop(0, chunks, gather_step, 0)
+    stage1(None)
+    lax.fori_loop(chunks, chunks + 1, gather_step, 0)
+    stage2(None)
+    lax.fori_loop(chunks + 1, chunks + 2, gather_step, 0)
+    stage3(None)
+
+    for k in range(2):
+        r = pl.ds(k * half, half)
+        v = acc[r, :]
+        hid[r, :] = (v / (1.0 + jnp.exp(-v))).astype(hid.dtype)
+    expert = core * (2 * major) + local
+    lane = lax.broadcasted_iota(jnp.int32, wg.shape, 1)
+    wcol[...] = jnp.sum(jnp.where(lane == expert, wg[...].astype(jnp.float32), 0.0), axis=1, keepdims=True)
+
+    def rp(j):
+        return remote(psend.at[:, cols(j)], precv.at[:, cols(j)], rp_s.at[j], rp_r.at[j], at_p)
+
+    def ry(j):
+        return remote(ysend.at[:, cols(j)], yrecv.at[:, cols(j)], ry_s.at[j], ry_r.at[j], at_y)
+
+    def rz(d, j):
+        src = zsend.at[pl.ds(pl.multiple_of(lax.rem(z + d, major) * rows, rows), rows), cols(j)]
+        return remote(src, zrecv.at[d - 1, :, cols(j)], rz_s.at[d - 1, j], rz_r.at[d - 1, j], at_z(d))
+
+    theirs = pl.ds(pl.multiple_of((1 - core) * half, half), half)
+    ours = pl.ds(pl.multiple_of(core * half, half), half)
+    y_theirs = pl.ds(pl.multiple_of((1 - y) * col_rows, col_rows), col_rows)
+    y_ours = pl.ds(pl.multiple_of(y * col_rows, col_rows), col_rows)
+    z_ours = pl.ds(pl.multiple_of(z * rows, rows), rows)
+
+    def scatter_step(t, _):
+        @pl.when(t < chunks)
+        def _():
+            j = t
+            down_copy(j).wait()
+            part = jnp.dot(hid[theirs, :], down[:, cols(j)], preferred_element_type=jnp.float32)
+            psend[:, cols(j)] = (part * wcol[theirs, :]).astype(psend.dtype)
+            rp(j).start()
+            part = jnp.dot(hid[ours, :], down[:, cols(j)], preferred_element_type=jnp.float32)
+            pown[:, cols(j)] = part * wcol[ours, :]
+
+        @pl.when((t >= 1) & (t <= chunks))
+        def _():
+            j = t - 1
+            rp(j).wait_recv()
+            ysend[:, cols(j)] = (pown[y_theirs, cols(j)] + precv[y_theirs, cols(j)].astype(jnp.float32)).astype(ysend.dtype)
+            ry(j).start()
+            yown[:, cols(j)] = pown[y_ours, cols(j)] + precv[y_ours, cols(j)].astype(jnp.float32)
+
+        @pl.when((t >= 2) & (t <= chunks + 1))
+        def _():
+            j = t - 2
+            ry(j).wait_recv()
+            zsend[:, cols(j)] = (yown[:, cols(j)] + yrecv[:, cols(j)].astype(jnp.float32)).astype(zsend.dtype)
+            for d in range(1, major):
+                rz(d, j).start()
+            zown[:, cols(j)] = yown[z_ours, cols(j)] + yrecv[z_ours, cols(j)].astype(jnp.float32)
+
+        @pl.when(t >= 3)
+        def _():
+            j = t - 3
+            total = zown[:, cols(j)]
+            for d in range(1, major):
+                rz(d, j).wait_recv()
+                total = total + zrecv[d - 1, :, cols(j)].astype(jnp.float32)
+            out_ref[:, cols(j)] = total.astype(out_ref.dtype)
+        return 0
+
+    lax.fori_loop(0, chunks + 3, scatter_step, 0)
+
+    def drain_gather(j):
+        for d in range(1, major):
+            gz_send(d, j).wait_send()
+        gy(y, j).wait_send()
+        gp(0, core, y, j).wait_send()
+        gp(1, core, 1 - y, j).wait_send()
+
+    def drain(j, _):
+        drain_gather(j)
+        rp(j).wait_send()
+        ry(j).wait_send()
+        for d in range(1, major):
+            rz(d, j).wait_send()
+        return 0
+
+    drain_gather(None)
+    lax.fori_loop(0, chunks, drain, 0)
+
+
+def fused(tokens, expert_ids, route_weights, w_up, w_down, width=512):
+    rows, depth = tokens.shape
+    ff = w_up.shape[2]
+    experts = lax.axis_size(("node", "local"))
+    major = lax.axis_size("local") // 2
+    chunks = depth // width
+    lanes = -(-experts // LANES) * LANES
+    hit = expert_ids[:, :, None] == jnp.arange(lanes, dtype=jnp.int32)
+    dense = jnp.sum(jnp.where(hit, route_weights[:, :, None].astype(jnp.float32), 0.0), axis=1).astype(jnp.bfloat16)
+    total, col = experts * rows, major * rows
+    half = 2 * col
+    bf, f32 = jnp.bfloat16, jnp.float32
+    dma = pltpu.SemaphoreType.DMA
+    return pl.pallas_call(
+        functools.partial(moe_kernel, (rows, major, chunks, width)),
+        out_shape=jax.ShapeDtypeStruct((rows, depth), bf),
+        in_specs=[pl.BlockSpec(memory_space=pl.ANY)] * 4,
+        out_specs=pl.BlockSpec(memory_space=pltpu.VMEM),
+        scratch_shapes=[
+            pltpu.VMEM((total, depth), bf),
+            pltpu.VMEM((total, lanes), bf),
+            pltpu.VMEM((depth, ff), bf),
+            pltpu.VMEM((ff, depth), bf),
+            pltpu.VMEM((total, ff), f32),
+            pltpu.VMEM((total, ff), bf),
+            pltpu.VMEM((total, 1), f32),
+            pltpu.VMEM((half, depth), bf),
+            pltpu.VMEM((half, depth), f32),
+            pltpu.VMEM((half, depth), bf),
+            pltpu.VMEM((col, depth), bf),
+            pltpu.VMEM((col, depth), f32),
+            pltpu.VMEM((col, depth), bf),
+            pltpu.VMEM((col, depth), bf),
+            pltpu.VMEM((rows, depth), f32),
+            pltpu.VMEM((major - 1, rows, depth), bf),
+            dma((2,)), dma((chunks,)), dma((chunks,)),
+            dma((major - 1, chunks + 1)), dma((major - 1, chunks + 1)),
+            dma((chunks + 1,)), dma((chunks + 1,)),
+            dma((2, chunks + 1)), dma((2, chunks + 1)),
+            dma((chunks,)), dma((chunks,)),
+            dma((chunks,)), dma((chunks,)),
+            dma((major - 1, chunks)), dma((major - 1, chunks)),
+        ],
+        compiler_params=pltpu.CompilerParams(
+            collective_id=0, has_side_effects=True, vmem_limit_bytes=60 * 1024 * 1024),
+    )(tokens, dense, w_up, w_down)
 
 
 def place_rows(targets, groups, width):
@@ -47,8 +316,16 @@
         P(("node", "local"), None, None),
         P(("node", "local"), None, None),
     )
+
+    def body(tokens, expert_ids, route_weights, w_up, w_down):
+        experts = mesh.shape["node"] * mesh.shape["local"]
+        near_dense = experts <= 2 * expert_ids.shape[1]
+        if near_dense and mesh.shape["node"] == 2 and mesh.shape["local"] % 4 == 0:
+            return fused(tokens, expert_ids, route_weights, w_up, w_down)
+        return per_device(tokens, expert_ids, route_weights, w_up, w_down)
+
     return jax.shard_map(
-        per_device,
+        body,
         mesh=mesh,
         in_specs=placed,
         out_specs=P(("rep", "node", "local"), None),

time: 215 us -> 76.3 us (0.35); the launches traced: 213 us -> 76.1 us
  blocking collectives: 90.7 us -> 0 us
  waiting for transfers between devices: 79.1 us -> 0 us
  Pallas kernels: 0 us -> 72.2 us
  matrix products: 16.6 us -> 0 us
  local copies, waits for them, and re-layouts: 19.3 us -> 3.16 us
  starting transfers between devices: 4.63 us -> 0 us
    all_to_all x1 -> x0, blocking collectives: 90.7 us -> none  [per_device(): lax.all_to_all(buffer, ('node', 'local'), split_axis=0, concat_axis=0, ti...]
    all_to_all x1 -> x0, waiting for transfers between devices: 79.1 us -> none  [per_device(): lax.all_to_all(done, ('node', 'local'), split_axis=0, concat_axis=0, tile...]
    pallas_call x0 -> x1, Pallas kernels: none -> 72.2 us  [fused(): pl.pallas_call(functools.partial(moe_kernel, (rows, major, chunks, width)...]
    dot_general x2 -> x0, matrix products: 16.6 us -> none  [the longest x1 16 us: per_device(): jnp.dot(hidden, down_matrix, preferred_element_type=jnp.float32)]
    scatter x1 -> x0, local copies, waits for them, and re-layouts: 10.9 us -> none  [per_device(): jnp.zeros((experts * most, width_d), jnp.bfloat16).at[slot]]
    gather x1 -> x0, local copies, waits for them, and re-layouts: 6.04 us -> none  [per_device(): returned[jnp.minimum(slot, experts * most - 1)].reshape(rows, top, width_d)]
    all_to_all x1 -> x0, starting transfers between devices: 4.63 us -> none  [per_device(): lax.all_to_all(done, ('node', 'local'), split_axis=0, concat_axis=0, tile...]
  transfers between devices with their start and end apart: 1 -> 0, of which waited for: 1 -> 0; matrix products, arithmetic and copies ran while one was open for 0% -> 0% of each run, Pallas kernels for 0% -> 0%
where the time goes in v1:
time: 76.3 us; the launch traced here: 76.1 us
  Pallas kernels  72.2 us (95%)
  local copies, waits for them, and re-layouts  3.16 us (4%)
    pallas_call x1, Pallas kernels, fused(): pl.pallas_call(functools.partial(moe_kernel, (rows, major, chunks, width)...  72.2 us
    unnamed x2, local copies, waits for them, and re-layouts  2.4 us

profile of v1, /device:TPU:0, one launch (start us, length us, event | category | flops | bytes accessed | tf_op | source)
XLA Modules:
  0.0 76.1 jit_solution(2154654523524998353)
XLA Ops:
  0.0 0.8 %copy.8 = s32[32,8]{1,0:T(8,128)S(1)} copy(s32[32,8]{0,1:T(8,128)} %param.6) | data formatting | bytes 2048 | tf_op args[1]
  0.8 0.8 copy.9
  1.5 0.8 select_reduce_fusion.dense_hbm
  2.3 72.2 %shard_map.55 = bf16[32,3584]{1,0:T(8,128)(2,1)} custom-call(bf16[32,3584]{1,0:T(8,128)(2,1)} %x_hbm.1, bf16[32,128]{1,0:T(8,128)(2,1)} %select_reduce_fusion.dense_hbm, bf16[1,3584,1024]{2,1,0:T(8,128)(2,1)} %up_hbm.1, bf16[1,1024,3584]{2,1,0:T(8,128)(2,1)} %down_hbm.1), custom_call_target="tpu_custom_call" | custom-call | tf_op jit(solution)/shard_map/pallas_call | solution.py:241
  74.4 1.6 %copy.11 = bf16[32,3584]{1,0:T(8,128)(2,1)} copy(bf16[32,3584]{1,0:T(8,128)(2,1)} %shard_map.55) | data formatting | bytes 458752

commit v2 on v1

--- a/solution.py
+++ b/solution.py
@@ -8,29 +8,36 @@
 
 MESH = pl.DeviceIdType.MESH
 LANES = 128
-
-
-def moe_kernel(sizes, x_hbm, dense_hbm, up_hbm, down_hbm, out_ref,
+LAG_A, LAG_B, LAG_D, LAG_F, LAG_G, LAG_R = 1, 3, 4, 1, 3, 5
+
+
+def moe_kernel(sizes, x_hbm, ids_ref, weights_ref, up_hbm, down_hbm, out_ref,
                xg, wg, up, down, acc, hid, wcol,
-               psend, pown, precv, ysend, yown, yrecv, zsend, zown, zrecv,
+               psend, pown, precv, ysend, yown, yrecv, zsend, zown, zrecv, rin,
                own_sem, up_sem, down_sem,
-               gz_s, gz_r, gy_s, gy_r, gp_s, gp_r,
-               rp_s, rp_r, ry_s, ry_r, rz_s, rz_r):
+               gz_s, gz_r, gr_s, go_s, go_r, gy_s, gy_r, gp_s, gp_r,
+               rp_s, rp_r, ro_s, ro_r, ry_s, ry_r, rz_s, rz_r, rr_s, rr_r):
     rows, major, chunks, width = sizes
     core = lax.axis_index("node")
     local = lax.axis_index("local")
     z, y = local // 2, lax.rem(local, 2)
+    last = major - 1
+    low, high = z == 0, z == last
+    inner = (z == 1) | (z == last - 1)
     col_rows = major * rows
     half = 2 * col_rows
 
-    def at_z(d):
-        return {"local": lax.rem(z + d, major) * 2 + y}
+    def z_plus(d):
+        return lax.rem(z + d, major)
+
+    def near(zz):
+        return {"local": zz * 2 + y}
 
     at_y = {"local": z * 2 + (1 - y)}
     at_p = {"node": 1 - core}
 
     barrier = pltpu.get_barrier_semaphore()
-    peers = [at_z(d) for d in range(1, major)] + [at_y, at_p]
+    peers = [near(z_plus(d)) for d in range(1, major)] + [at_y, at_p]
     for peer in peers:
         pl.semaphore_signal(barrier, inc=1, device_id=peer, device_id_type=MESH)
 
@@ -39,9 +46,7 @@
 
     mine = rows_of(core, y, z)
     own_x = pltpu.make_async_copy(x_hbm, xg.at[pl.ds(mine, rows), :], own_sem.at[0])
-    own_w = pltpu.make_async_copy(dense_hbm, wg.at[pl.ds(mine, rows), :], own_sem.at[1])
     own_x.start()
-    own_w.start()
 
     def cols(j):
         return pl.ds(pl.multiple_of(j * width, width), width)
@@ -55,8 +60,17 @@
     lax.fori_loop(0, chunks, lambda j, _: (up_copy(j).start(), 0)[1], 0)
     lax.fori_loop(0, chunks, lambda j, _: (down_copy(j).start(), 0)[1], 0)
 
+    lanes = wg.shape[1]
+    expert_row = lax.broadcasted_iota(jnp.int32, (lanes, rows), 0)
+    spread = jnp.zeros((lanes, rows), jnp.float32)
+    for k in range(ids_ref.shape[0]):
+        spread += jnp.where(expert_row == ids_ref[k:k + 1, :], weights_ref[k:k + 1, :].astype(jnp.float32), 0.0)
+    unit = (lax.broadcasted_iota(jnp.int32, (rows, rows), 0) == lax.broadcasted_iota(jnp.int32, (rows, rows), 1))
+    wg[pl.ds(mine, rows), :] = lax.dot_general(
+        unit.astype(jnp.float32).astype(jnp.bfloat16), spread.astype(jnp.bfloat16), (((1,), (1,)), ((), ())),
+        preferred_element_type=jnp.float32).astype(wg.dtype)
+
     own_x.wait()
-    own_w.wait()
     pl.semaphore_wait(barrier, len(peers))
 
     def view(start, size, j):
@@ -73,15 +87,35 @@
 
     def gz_send(d, j):
         v = view(mine, rows, j)
-        return remote(v, v, gz_s.at[d - 1, idx(j)], gz_r.at[d - 1, idx(j)], at_z(d))
+        return remote(v, v, gz_s.at[d - 1, idx(j)], gz_r.at[d - 1, idx(j)], near(z_plus(d)))
+
+    def direct(d, start):
+        if d == 1:
+            pl.when(jnp.logical_not(high))(start)
+        elif d == last:
+            pl.when(jnp.logical_not(low))(start)
+        else:
+            start()
 
     def gz_recv(d, j):
-        v = view(rows_of(core, y, lax.rem(z + major - d, major)), rows, j)
-        return remote(v, v, gz_s.at[d - 1, idx(j)], gz_r.at[d - 1, idx(j)], at_z(d))
-
-    def gy(which, j):
-        v = view(rows_of(core, which, 0), col_rows, j)
-        return remote(v, v, gy_s.at[idx(j)], gy_r.at[idx(j)], at_y)
+        v = view(rows_of(core, y, z_plus(major - d)), rows, j)
+        return remote(v, v, gz_s.at[d - 1, idx(j)], gz_r.at[d - 1, idx(j)], near(z_plus(1)))
+
+    far = jnp.where(z == 1, last, 0)
+    far_d = jnp.where(z == 1, 2, last - 1)
+
+    def relay(j):
+        v = view(rows_of(core, y, far), rows, j)
+        d = jnp.where(z == 1, 1, last)
+        return remote(v, v, gr_s.at[idx(j)], gz_r.at[d - 1, idx(j)], near(last - far))
+
+    def go(which, j):
+        v = view(rows_of(core, which, z), rows, j)
+        return remote(v, v, go_s.at[idx(j)], go_r.at[idx(j)], at_y)
+
+    def gy(d, which, j):
+        v = view(rows_of(core, which, z_plus(major - d)), rows, j)
+        return remote(v, v, gy_s.at[d - 1, idx(j)], gy_r.at[d - 1, idx(j)], at_y)
 
     def gp(k, c, which, j):
         v = view(rows_of(c, which, 0), col_rows, j)
@@ -89,16 +123,27 @@
 
     def stage0(j):
         for d in range(1, major):
-            gz_send(d, j).start()
+            direct(d, lambda: gz_send(d, j).start())
+        go(y, j).start()
+
+    def stage_relay(j):
+        @pl.when(inner)
+        def _():
+            gz_recv(far_d, j).wait_recv()
+            relay(j).start()
 
     def stage1(j):
         for d in range(1, major):
-            gz_recv(d, j).wait_recv()
-        gy(y, j).start()
+            @pl.when(jnp.logical_not(inner & (far_d == d)))
+            def _():
+                gz_recv(d, j).wait_recv()
+            gy(d, y, j).start()
         gp(0, core, y, j).start()
 
     def stage2(j):
-        gy(1 - y, j).wait_recv()
+        go(1 - y, j).wait_recv()
+        for d in range(1, major):
+            gy(d, 1 - y, j).wait_recv()
         gp(1, core, 1 - y, j).start()
 
     def stage3(j):
@@ -111,15 +156,19 @@
     def gather_step(t, _):
         @pl.when(t < chunks)
         def _():
-            stage1(t)
-
-        @pl.when((t >= 1) & (t <= chunks))
-        def _():
-            stage2(t - 1)
-
-        @pl.when(t >= 2)
-        def _():
-            j = t - 2
+            stage_relay(t)
+
+        @pl.when((t >= LAG_A) & (t < chunks + LAG_A))
+        def _():
+            stage1(t - LAG_A)
+
+        @pl.when((t >= LAG_B) & (t < chunks + LAG_B))
+        def _():
+            stage2(t - LAG_B)
+
+        @pl.when(t >= LAG_D)
+        def _():
+            j = t - LAG_D
             stage3(j)
             up_copy(j).wait()
             for k in range(2):
@@ -136,10 +185,12 @@
         return 0
 
     lax.fori_loop(0, chunks, gather_step, 0)
+    stage_relay(None)
+    lax.fori_loop(chunks, chunks + LAG_A, gather_step, 0)
     stage1(None)
-    lax.fori_loop(chunks, chunks + 1, gather_step, 0)
+    lax.fori_loop(chunks + LAG_A, chunks + LAG_B, gather_step, 0)
     stage2(None)
-    lax.fori_loop(chunks + 1, chunks + 2, gather_step, 0)
+    lax.fori_loop(chunks + LAG_B, chunks + LAG_D, gather_step, 0)
     stage3(None)
 
     for k in range(2):
@@ -150,21 +201,38 @@
     lane = lax.broadcasted_iota(jnp.int32, wg.shape, 1)
     wcol[...] = jnp.sum(jnp.where(lane == expert, wg[...].astype(jnp.float32), 0.0), axis=1, keepdims=True)
 
+    def block(zz):
+        return pl.ds(pl.multiple_of(zz * rows, rows), rows)
+
     def rp(j):
         return remote(psend.at[:, cols(j)], precv.at[:, cols(j)], rp_s.at[j], rp_r.at[j], at_p)
 
-    def ry(j):
-        return remote(ysend.at[:, cols(j)], yrecv.at[:, cols(j)], ry_s.at[j], ry_r.at[j], at_y)
+    def ry(d, j):
+        r = block(z_plus(d))
+        return remote(ysend.at[r, cols(j)], yrecv.at[r, cols(j)], ry_s.at[d - 1, j], ry_r.at[d - 1, j], at_y)
+
+    def ro(j):
+        return remote(ysend.at[block(z), cols(j)], yrecv.at[block(z), cols(j)], ro_s.at[j], ro_r.at[j], at_y)
 
     def rz(d, j):
-        src = zsend.at[pl.ds(pl.multiple_of(lax.rem(z + d, major) * rows, rows), rows), cols(j)]
-        return remote(src, zrecv.at[d - 1, :, cols(j)], rz_s.at[d - 1, j], rz_r.at[d - 1, j], at_z(d))
+        return remote(zsend.at[block(z_plus(d)), cols(j)], zrecv.at[d - 1, :, cols(j)],
+                      rz_s.at[d - 1, j], rz_r.at[d - 1, j], near(z_plus(d)))
+
+    target = last - z
+    via = jnp.where(low, 1, last - 1)
+    skip_d = jnp.where(z == 1, last - 1, 2)
+    goal = jnp.where(z == 1, last, 0)
+
+    def rr(j):
+        return remote(zsend.at[block(target), cols(j)], rin.at[:, cols(j)], rr_s.at[j], rr_r.at[j], near(via))
 
     theirs = pl.ds(pl.multiple_of((1 - core) * half, half), half)
     ours = pl.ds(pl.multiple_of(core * half, half), half)
     y_theirs = pl.ds(pl.multiple_of((1 - y) * col_rows, col_rows), col_rows)
     y_ours = pl.ds(pl.multiple_of(y * col_rows, col_rows), col_rows)
-    z_ours = pl.ds(pl.multiple_of(z * rows, rows), rows)
+
+    def wide(ref, r, j):
+        return ref[r, cols(j)].astype(jnp.float32)
 
     def scatter_step(t, _):
         @pl.when(t < chunks)
@@ -177,48 +245,90 @@
             part = jnp.dot(hid[ours, :], down[:, cols(j)], preferred_element_type=jnp.float32)
             pown[:, cols(j)] = part * wcol[ours, :]
 
-        @pl.when((t >= 1) & (t <= chunks))
-        def _():
-            j = t - 1
+        @pl.when((t >= LAG_F) & (t < chunks + LAG_F))
+        def _():
+            j = t - LAG_F
             rp(j).wait_recv()
-            ysend[:, cols(j)] = (pown[y_theirs, cols(j)] + precv[y_theirs, cols(j)].astype(jnp.float32)).astype(ysend.dtype)
-            ry(j).start()
-            yown[:, cols(j)] = pown[y_ours, cols(j)] + precv[y_ours, cols(j)].astype(jnp.float32)
-
-        @pl.when((t >= 2) & (t <= chunks + 1))
-        def _():
-            j = t - 2
-            ry(j).wait_recv()
-            zsend[:, cols(j)] = (yown[:, cols(j)] + yrecv[:, cols(j)].astype(jnp.float32)).astype(zsend.dtype)
+            ysend[:, cols(j)] = (pown[y_theirs, cols(j)] + wide(precv, y_theirs, j)).astype(ysend.dtype)
             for d in range(1, major):
-                rz(d, j).start()
-            zown[:, cols(j)] = yown[z_ours, cols(j)] + yrecv[z_ours, cols(j)].astype(jnp.float32)
-
-        @pl.when(t >= 3)
-        def _():
-            j = t - 3
-            total = zown[:, cols(j)]
+                ry(d, j).start()
+            yown[:, cols(j)] = pown[y_ours, cols(j)] + wide(precv, y_ours, j)
+
+        @pl.when(t == chunks + LAG_F - 1)
+        def _():
+            lax.fori_loop(0, chunks, lambda i, _: (ro(i).start(), 0)[1], 0)
+
+        @pl.when((t >= LAG_G) & (t < chunks + LAG_G))
+        def _():
+            j = t - LAG_G
             for d in range(1, major):
+                ry(d, j).wait_recv()
+                r = block(z_plus(d))
+                zsend[r, cols(j)] = (yown[r, cols(j)] + wide(yrecv, r, j)).astype(zsend.dtype)
+
+            @pl.when(low | high)
+            def _():
+                rr(j).start()
+            for d in range(1, major):
+                @pl.when(jnp.logical_not(inner & (skip_d == d)))
+                def _():
+                    direct(d, lambda: rz(d, j).start())
+
+        @pl.when(inner & (t >= LAG_R) & (t < chunks + LAG_R))
+        def _():
+            j = t - LAG_R
+            rr(j).wait_recv()
+            zsend[block(goal), cols(j)] = (
+                wide(zsend, block(goal), j) + rin[:, cols(j)].astype(jnp.float32)).astype(zsend.dtype)
+            for d in range(1, major):
+                @pl.when(skip_d == d)
+                def _():
+                    rz(d, j).start()
+        return 0
+
+    lax.fori_loop(0, chunks + LAG_R, scatter_step, 0)
+
+    def finish(j, _):
+        ro(j).wait_recv()
+        zown[...] = yown[block(z), cols(j)] + wide(yrecv, block(z), j)
+        for d in range(1, major):
+            def add():
                 rz(d, j).wait_recv()
-                total = total + zrecv[d - 1, :, cols(j)].astype(jnp.float32)
-            out_ref[:, cols(j)] = total.astype(out_ref.dtype)
+                zown[...] += zrecv[d - 1, :, cols(j)].astype(jnp.float32)
+            if d == 1:
+                pl.when(jnp.logical_not(low))(add)
+            elif d == last:
+                pl.when(jnp.logical_not(high))(add)
+            else:
+                add()
+        out_ref[:, cols(j)] = zown[...].astype(out_ref.dtype)
         return 0
 
-    lax.fori_loop(0, chunks + 3, scatter_step, 0)
+    lax.fori_loop(0, chunks, finish, 0)
 
     def drain_gather(j):
         for d in range(1, major):
-            gz_send(d, j).wait_send()
-        gy(y, j).wait_send()
+            direct(d, lambda: gz_send(d, j).wait_send())
+            gy(d, y, j).wait_send()
+
+        @pl.when(inner)
+        def _():
+            relay(j).wait_send()
+        go(y, j).wait_send()
         gp(0, core, y, j).wait_send()
         gp(1, core, 1 - y, j).wait_send()
 
     def drain(j, _):
         drain_gather(j)
         rp(j).wait_send()
-        ry(j).wait_send()
-        for d in range(1, major):
-            rz(d, j).wait_send()
+        ro(j).wait_send()
+        for d in range(1, major):
+            ry(d, j).wait_send()
+            direct(d, lambda: rz(d, j).wait_send())
+
+        @pl.when(low | high)
+        def _():
+            rr(j).wait_send()
         return 0
 
     drain_gather(None)
@@ -232,8 +342,6 @@
     major = lax.axis_size("local") // 2
     chunks = depth // width
     lanes = -(-experts // LANES) * LANES
-    hit = expert_ids[:, :, None] == jnp.arange(lanes, dtype=jnp.int32)
-    dense = jnp.sum(jnp.where(hit, route_weights[:, :, None].astype(jnp.float32), 0.0), axis=1).astype(jnp.bfloat16)
     total, col = experts * rows, major * rows
     half = 2 * col
     bf, f32 = jnp.bfloat16, jnp.float32
@@ -241,7 +349,13 @@
     return pl.pallas_call(
         functools.partial(moe_kernel, (rows, major, chunks, width)),
         out_shape=jax.ShapeDtypeStruct((rows, depth), bf),
-        in_specs=[pl.BlockSpec(memory_space=pl.ANY)] * 4,
+        in_specs=[
+            pl.BlockSpec(memory_space=pl.ANY),
+            pl.BlockSpec(memory_space=pltpu.VMEM),
+            pl.BlockSpec(memory_space=pltpu.VMEM),
+            pl.BlockSpec(memory_space=pl.ANY),
+            pl.BlockSpec(memory_space=pl.ANY),
+        ],
         out_specs=pl.BlockSpec(memory_space=pltpu.VMEM),
         scratch_shapes=[
             pltpu.VMEM((total, depth), bf),
@@ -258,19 +372,23 @@
             pltpu.VMEM((col, depth), f32),
             pltpu.VMEM((col, depth), bf),
             pltpu.VMEM((col, depth), bf),
-            pltpu.VMEM((rows, depth), f32),
+            pltpu.VMEM((rows, width), f32),
             pltpu.VMEM((major - 1, rows, depth), bf),
-            dma((2,)), dma((chunks,)), dma((chunks,)),
+            pltpu.VMEM((rows, depth), bf),
+            dma((1,)), dma((chunks,)), dma((chunks,)),
+            dma((major - 1, chunks + 1)), dma((major - 1, chunks + 1)), dma((chunks + 1,)),
+            dma((chunks + 1,)), dma((chunks + 1,)),
             dma((major - 1, chunks + 1)), dma((major - 1, chunks + 1)),
-            dma((chunks + 1,)), dma((chunks + 1,)),
             dma((2, chunks + 1)), dma((2, chunks + 1)),
             dma((chunks,)), dma((chunks,)),
             dma((chunks,)), dma((chunks,)),
             dma((major - 1, chunks)), dma((major - 1, chunks)),
+            dma((major - 1, chunks)), dma((major - 1, chunks)),
+            dma((chunks,)), dma((chunks,)),
         ],
         compiler_params=pltpu.CompilerParams(
             collective_id=0, has_side_effects=True, vmem_limit_bytes=60 * 1024 * 1024),
-    )(tokens, dense, w_up, w_down)
+    )(tokens, expert_ids.T, route_weights.T, w_up, w_down)
 
 
 def place_rows(targets, groups, width):
@@ -320,7 +438,7 @@
     def body(tokens, expert_ids, route_weights, w_up, w_down):
         experts = mesh.shape["node"] * mesh.shape["local"]
         near_dense = experts <= 2 * expert_ids.shape[1]
-        if near_dense and mesh.shape["node"] == 2 and mesh.shape["local"] % 4 == 0:
+        if near_dense and mesh.shape["node"] == 2 and mesh.shape["local"] % 2 == 0 and mesh.shape["local"] >= 8:
             return fused(tokens, expert_ids, route_weights, w_up, w_down)
         return per_device(tokens, expert_ids, route_weights, w_up, w_down)
 

time: 76.3 us -> 63.4 us (0.83)
  Pallas kernels: 72.2 us -> 61.6 us
  local copies, waits for them, and re-layouts: 3.16 us -> 1.64 us
    pallas_call x1, Pallas kernels: 72.2 us -> 61.6 us  [fused(): pl.pallas_call(functools.partial(moe_kernel, (rows, major, chunks, width)...]
    unnamed x2 -> x1, local copies, waits for them, and re-layouts: 2.4 us -> 1.64 us
where the time goes in v2:
time: 63.4 us; the launch traced here: 63.2 us
  Pallas kernels  61.6 us (97%)
  local copies, waits for them, and re-layouts  1.64 us (3%)
    pallas_call x1, Pallas kernels, fused(): pl.pallas_call(functools.partial(moe_kernel, (rows, major, chunks, width)...  61.6 us
    unnamed x1, local copies, waits for them, and re-layouts  1.64 us

profile of v2, /device:TPU:0, one launch (start us, length us, event | category | flops | bytes accessed | tf_op | source)
XLA Modules:
  0.0 63.2 jit_solution(14319995966365619924)
XLA Ops:
  0.0 61.6 %shard_map.55 = bf16[32,3584]{1,0:T(8,128)(2,1)} custom-call(bf16[32,3584]{1,0:T(8,128)(2,1)} %x_hbm.1, s32[8,32]{1,0:T(8,128)} %bitcast.2, bf16[8,32]{1,0:T(8,128)(2,1)} %bitcast.3, bf16[1,3584,1024]{2,1,0:T(8,128)(2,1)} %up_hbm.1, bf16[1,1024,3584]{2,1,0:T(8,128)(2,1)} %down_hbm.1), custom_call_target="tpu_custom_call" | custom-call | tf_op jit(solution)/shard_map/pallas_call | solution.py:349
  61.6 1.6 %copy.7 = bf16[32,3584]{1,0:T(8,128)(2,1)} copy(bf16[32,3584]{1,0:T(8,128)(2,1)} %shard_map.55) | data formatting | bytes 458752

commit v3 on v2

--- a/solution.py
+++ b/solution.py
@@ -8,7 +8,8 @@
 
 MESH = pl.DeviceIdType.MESH
 LANES = 128
-LAG_A, LAG_B, LAG_D, LAG_F, LAG_G, LAG_R = 1, 3, 4, 1, 3, 5
+LAG_A, LAG_B, LAG_D, LAG_F, LAG_G, LAG_R = 1, 4, 5, 1, 4, 7
+AHEAD = 3
 
 
 def moe_kernel(sizes, x_hbm, ids_ref, weights_ref, up_hbm, down_hbm, out_ref,
@@ -122,9 +123,8 @@
         return remote(v, v, gp_s.at[k, idx(j)], gp_r.at[k, idx(j)], at_p)
 
     def stage0(j):
-        for d in range(1, major):
+        for d in (*range(2, last), 1, last):
             direct(d, lambda: gz_send(d, j).start())
-        go(y, j).start()
 
     def stage_relay(j):
         @pl.when(inner)
@@ -150,10 +150,16 @@
         gp(0, 1 - core, y, j).wait_recv()
         gp(1, 1 - core, 1 - y, j).wait_recv()
 
-    lax.fori_loop(0, chunks, lambda j, _: (stage0(j), 0)[1], 0)
+    lax.fori_loop(0, AHEAD, lambda j, _: (stage0(j), 0)[1], 0)
+    lax.fori_loop(0, chunks, lambda j, _: (go(y, j).start(), 0)[1], 0)
     stage0(None)
+    go(y, None).start()
 
     def gather_step(t, _):
+        @pl.when(t + AHEAD < chunks)
+        def _():
+            stage0(t + AHEAD)
+
         @pl.when(t < chunks)
         def _():
             stage_relay(t)
@@ -348,7 +354,7 @@
     dma = pltpu.SemaphoreType.DMA
     return pl.pallas_call(
         functools.partial(moe_kernel, (rows, major, chunks, width)),
-        out_shape=jax.ShapeDtypeStruct((rows, depth), bf),
+        out_shape=pltpu.VMEM((rows, depth), bf),
         in_specs=[
             pl.BlockSpec(memory_space=pl.ANY),
             pl.BlockSpec(memory_space=pltpu.VMEM),

time: 63.4 us -> 59.9 us (0.945)
  Pallas kernels: 61.6 us -> 59.1 us
  local copies, waits for them, and re-layouts: 1.64 us -> 0.69 us
    pallas_call x1, Pallas kernels: 61.6 us -> 59.1 us  [fused(): pl.pallas_call(functools.partial(moe_kernel, (rows, major, chunks, width)...]
    unnamed x1, local copies, waits for them, and re-layouts: 1.64 us -> 0.69 us
where the time goes in v3:
time: 59.9 us; the launch traced here: 59.8 us
  Pallas kernels  59.1 us (99%)
  local copies, waits for them, and re-layouts  0.69 us (1%)
    pallas_call x1, Pallas kernels, fused(): pl.pallas_call(functools.partial(moe_kernel, (rows, major, chunks, width)...  59.1 us

profile of v3, /device:TPU:0, one launch (start us, length us, event | category | flops | bytes accessed | tf_op | source)
XLA Modules:
  0.0 59.8 jit_solution(12389131259999789891)
XLA Ops:
  0.0 59.1 %shard_map.55 = bf16[32,3584]{1,0:T(8,128)(2,1)S(1)} custom-call(bf16[32,3584]{1,0:T(8,128)(2,1)} %x_hbm.1, s32[8,32]{1,0:T(8,128)} %bitcast.2, bf16[8,32]{1,0:T(8,128)(2,1)} %bitcast.3, bf16[1,3584,1024]{2,1,0:T(8,128)(2,1)} %up_hbm.1, bf16[1,1024,3584]{2,1,0:T(8,128)(2,1)} %down_hbm.1), custom_call_target="tpu_custom_call" | custom-call | tf_op jit(solution)/shard_map/pallas_call | solution.py:355
  59.1 0.7 %copy.7 = bf16[32,3584]{1,0:T(8,128)(2,1)} copy(bf16[32,3584]{1,0:T(8,128)(2,1)S(1)} %shard_map.55) | data formatting | bytes 458752
